TPU v7x, 128 devices: a whole 4x4x4 slice. The times are simulated.
128 devices in a mesh: row: 16 (over y, z), col: 8 (over x, core).
Axes of the slice: x: 4, y: 4, z: 4, core: 2. Of those that a mesh axis runs over, the one named last changes fastest.
Arguments:
- kernel_rows: float32 [2, 16, 8, 64, 16384], P(None, 'row', 'col'), may hold values from -1 to 8, as said below
Outputs:
- factored: float32 [2, 16, 512, 4, 8, 512], P(None, 'row', None, None, 'col')
Inputs may be any that keep to these rules, and one draw needn't show every extreme that they name: `kernel_rows`: the matrix A that the rows make is symmetric and positive definite.
All inputs are finite; a program needn't handle non-finite values.
Results may differ from a plain program's by a relative error of at most 0.0001.
Values sent between devices are 32-bit elements; how exact they have to be, the bound alone decides.
A program may use at most 128 MiB of HBM per device.

v0:
```python
import jax
import jax.numpy as jnp
from jax import lax
from jax.sharding import PartitionSpec as P


def spread(block, axis, owner):
    block = jnp.where(lax.axis_index(axis) == owner, block, jnp.zeros_like(block))
    return lax.psum(block, axis)


def solve_rows(factor_tile, column):
    row_tiles, tile_size = (column.shape[0], column.shape[1])
    stacked = column.reshape(row_tiles * tile_size, tile_size)
    solved = jax.scipy.linalg.solve_triangular(factor_tile, stacked.T, lower=True)
    return solved.T.reshape(row_tiles, tile_size, tile_size)


def factor(tiles_here, panel_idx, grid_rows, grid_cols):
    row_at, col_at = (panel_idx // grid_rows, panel_idx // grid_cols)
    row_root, col_root = (panel_idx % grid_rows, panel_idx % grid_cols)
    column = tiles_here[:, :, col_at, :]
    diag_piece = tiles_here[row_at, :, col_at, :]
    diag_tile = spread(diag_piece, "row", row_root)
    factor_tile = jnp.linalg.cholesky(diag_tile)
    solved = spread(solve_rows(factor_tile, column), "col", col_root)
    return (factor_tile, solved)


def mirror(solved, grid_rows, grid_cols):
    pieces = []
    for copy_idx in range(grid_rows // grid_cols):
        root_row = lax.axis_index("col") + copy_idx * grid_cols
        pieces.append(spread(solved, "row", root_row))
    row_tiles, tile_size = (solved.shape[0], solved.shape[1])
    return jnp.stack(pieces, axis=1).reshape(-1, tile_size, tile_size)


def update(
    tiles_here, panel_idx, factor_tile, solved, col_factor, row_ids, col_ids, grid_rows, grid_cols
):
    left_part = jnp.where((row_ids > panel_idx)[:, None, None], solved, jnp.float32(0.0))
    right_part = jnp.where((col_ids > panel_idx)[:, None, None], col_factor, jnp.float32(0.0))
    tiles_here = tiles_here - jnp.einsum(
        "aur,bvr->aubv", left_part, right_part, precision=lax.Precision.HIGHEST
    )
    row_at, col_at = (panel_idx // grid_rows, panel_idx // grid_cols)
    row_root, col_root = (panel_idx % grid_rows, panel_idx % grid_cols)
    below_mask = (row_ids > panel_idx)[:, None, None]
    diag_mask = (row_ids == panel_idx)[:, None, None]
    col_values = jnp.where(
        below_mask, solved, jnp.where(diag_mask, factor_tile[None], jnp.float32(0.0))
    )
    owner_col = lax.axis_index("col") == col_root
    tiles_here = tiles_here.at[:, :, col_at, :].set(
        jnp.where(owner_col, col_values, tiles_here[:, :, col_at, :])
    )
    zero_mask = (lax.axis_index("row") == row_root) & (col_ids > panel_idx)
    tiles_here = tiles_here.at[row_at].set(
        jnp.where(zero_mask[None, :, None], jnp.float32(0.0), tiles_here[row_at])
    )
    return tiles_here


def shards(kernel_rows):
    grid_rows = lax.axis_size("row")
    grid_cols = lax.axis_size("col")
    row_tiles, sub_rows, mat_order = (
        kernel_rows.shape[0],
        kernel_rows.shape[3],
        kernel_rows.shape[4],
    )
    tile_size = sub_rows * grid_cols
    col_tiles = mat_order // (tile_size * grid_cols)
    shaped = kernel_rows.reshape(row_tiles, sub_rows, col_tiles, grid_cols, tile_size)
    placed = lax.all_to_all(shaped, "col", split_axis=3, concat_axis=1, tiled=True)
    tiles_here = placed.reshape(row_tiles, tile_size, col_tiles, tile_size)
    row_ids = jnp.arange(row_tiles, dtype=jnp.int32) * grid_rows + lax.axis_index("row")
    col_ids = jnp.arange(col_tiles, dtype=jnp.int32) * grid_cols + lax.axis_index("col")
    for panel_idx in range(2):
        factor_tile, solved = factor(tiles_here, panel_idx, grid_rows, grid_cols)
        col_factor = mirror(solved, grid_rows, grid_cols)
        tiles_here = update(
            tiles_here,
            panel_idx,
            factor_tile,
            solved,
            col_factor,
            row_ids,
            col_ids,
            grid_rows,
            grid_cols,
        )
    return tiles_here.reshape(row_tiles, 1, tile_size, col_tiles, 1, tile_size)


def solution(mesh):
    return jax.shard_map(
        shards,
        mesh=mesh,
        in_specs=(P(None, "row", "col", None, None),),
        out_specs=P(None, "row", None, None, "col", None),
        check_vma=False,
    )
```

profile of v0, /device:TPU:1, one launch (start us, length us, event | category | flops | bytes accessed | tf_op | source)
XLA Modules:
  0.0 1100.3 jit_solution(1424373501177448121)
XLA Ops:
  6.5 13.3 %copy.99 = f32[16,8,32,512]{3,2,1,0:T(8,128)} copy(f32[16,8,32,512]{3,1,2,0:T(8,128)} %bitcast.198) | data formatting | bytes 16777216
  19.8 23.6 %copy.63 = f32[2,64,4,8,512]{4,2,1,0,3:T(4,128)} copy(f32[2,64,4,8,512]{4,3,2,1,0:T(8,128)} %bitcast.197) | data formatting | bytes 16777216 | tf_op jit(solution)/shard_map/reshape | solution.py:75
  43.4 6.2 all-to-all-start
  49.6 93.7 %all-to-all-done = f32[2,64,4,8,512]{4,2,1,0,3:T(4,128)} async-done(((f32[2,64,4,8,512]{4,2,1,0,3:T(4,128)}), f32[2,64,4,8,512]{4,2,1,0,3:T(4,128)}, u32[]{:S(2)}, u32[]{:S(2)}) %all-to-all-start) | async-done | bytes 8388640 | tf_op jit(solution)/shard_map/all_to_all | solution.py:76
  159.2 82.0 %all-reduce.10.cloned.1.call-done = f32[512,512]{0,1:T(8,128)} async-done(((f32[512,512]{0,1:T(8,128)}), f32[512,512]{0,1:T(8,128)}) %all-reduce.10.cloned.1.call-update) | async-done | bytes 1048592 | tf_op jit(solution)/shard_map/psum | solution.py:9
  246.3 11.7 %cholesky.286 = f32[128,128]{1,0:T(8,128)S(1)} custom-call(f32[128,128]{1,0:T(8,128)S(1)} %cholesky.426), custom_call_target="Cholesky" | custom-call | tf_op jit(solution)/shard_map/jit(cholesky)/cholesky | solution.py:25
  258.1 9.8 custom-call.27
  270.6 11.7 %cholesky.305 = f32[128,128]{1,0:T(8,128)S(1)} custom-call(f32[128,128]{1,0:T(8,128)S(1)} %cholesky.430), custom_call_target="Cholesky" | custom-call | tf_op jit(solution)/shard_map/jit(cholesky)/cholesky | solution.py:25
  282.3 10.2 custom-call.28
  294.1 11.7 %cholesky.326 = f32[128,128]{1,0:T(8,128)S(1)} custom-call(f32[128,128]{1,0:T(8,128)S(1)} %cholesky.435), custom_call_target="Cholesky" | custom-call | tf_op jit(solution)/shard_map/jit(cholesky)/cholesky | solution.py:25
  306.5 9.8 custom-call.29
  317.8 11.7 %cholesky.343 = f32[128,128]{1,0:T(8,128)S(1)} custom-call(f32[128,128]{1,0:T(8,128)S(1)} %convolution_subtract_fusion.9), custom_call_target="Cholesky" | custom-call | tf_op jit(solution)/shard_map/jit(cholesky)/cholesky | solution.py:25
  335.3 11.7 %while.8 = (s32[]{:T(128)}, f32[512,512]{1,0:T(8,128)}, s32[4,2]{0,1:T(2,128)S(1)}, f32[4,128,128]{2,1,0:T(8,128)S(1)}, s32[]{:T(128)}) while((s32[]{:T(128)}, f32[512,512]{1,0:T(8,128)}, s32[4,2]{0,1:T(2,128)S(1)}, f32[4,128,128]{2,1,0:T(8,128)S(1)}, s32[]{:T(128)}) %tuple.74), condition=%wide.while_cond.4, body=%wide.while_body.4.sunk | while | flops 2 | bytes 131181 | solution.py:15
  347.0 39.3 %custom-call.30 = f32[4,128,128]{1,2,0:T(8,128)S(1)} custom-call(f32[4,128,128]{2,1,0:T(8,128)S(1)} %get-tuple-element.69), custom_call_target="InvertDiagBlocksLowerTriangular" | custom-call | tf_op jit(solution)/shard_map/jit(_solve_triangular)/triangular_solve | solution.py:15
  399.0 64.5 %all-reduce.12.cloned.1.call-done = f32[2,512,512]{1,2,0:T(8,128)} async-done(((f32[2,512,512]{1,2,0:T(8,128)}), f32[2,512,512]{1,2,0:T(8,128)}) %all-reduce.12.cloned.1.call-update) | async-done | bytes 2097168 | tf_op jit(solution)/shard_map/psum | solution.py:9
  467.9 10.2 copy.72
  478.4 94.4 %all-reduce.20.cloned.1.call-done = (f32[2,1,512,512]{2,3,0,1:T(8,128)}, f32[2,1,512,512]{2,3,0,1:T(8,128)}) async-done(((f32[2,1,512,512]{2,3,0,1:T(8,128)}, f32[2,1,512,512]{2,3,0,1:T(8,128)}), (f32[2,1,512,512]{2,3,0,1:T(8,128)}, f32[2,1,512,512]{2,3,0,1:T(8,128)})) %all-reduce.20.cloned.1.call-update) | async-done | bytes 4194320 | tf_op jit(solution)/shard_map/psum | solution.py:9
  585.9 18.0 %fusion.10 = f32[2,512,4,512]{1,3,0,2:T(8,128)S(1)} fusion(f32[2,512,4,512]{1,3,0,2:T(8,128)} %copy.72, f32[4,512,512]{2,1,0:T(8,128)S(1)} %bitcast_select_fusion.1, f32[2,512,512]{1,2,0:T(8,128)S(1)} %copy-done.1, pred[2]{0:T(512)(128)(4,1)S(1)} %get-tuple-element.130), kind=kOutput, calls=%fused_computation.18 | convolution fusion | flops 12887523328 | bytes 23068674 | tf_op jit(solution)/shard_map/aur,bvr->aubv/dot_general | solution.py:44
  622.5 80.2 %all-reduce.14.cloned.1.call-done = f32[512,512]{0,1:T(8,128)} async-done(((f32[512,512]{0,1:T(8,128)}), f32[512,512]{0,1:T(8,128)}) %all-reduce.14.cloned.1.call-update) | async-done | bytes 1048592 | tf_op jit(solution)/shard_map/psum | solution.py:9
  707.9 11.7 %cholesky.358 = f32[128,128]{1,0:T(8,128)S(1)} custom-call(f32[128,128]{1,0:T(8,128)S(1)} %cholesky.439), custom_call_target="Cholesky" | custom-call | tf_op jit(solution)/shard_map/jit(cholesky)/cholesky | solution.py:25
  719.7 9.8 custom-call.31
  732.1 11.7 %cholesky.377 = f32[128,128]{1,0:T(8,128)S(1)} custom-call(f32[128,128]{1,0:T(8,128)S(1)} %cholesky.443), custom_call_target="Cholesky" | custom-call | tf_op jit(solution)/shard_map/jit(cholesky)/cholesky | solution.py:25
  745.2 10.0 custom-call.32
  756.7 11.7 %cholesky.398 = f32[128,128]{1,0:T(8,128)S(1)} custom-call(f32[128,128]{1,0:T(8,128)S(1)} %cholesky.448), custom_call_target="Cholesky" | custom-call | tf_op jit(solution)/shard_map/jit(cholesky)/cholesky | solution.py:25
  769.1 9.8 custom-call.33
  780.4 11.7 %cholesky.415 = f32[128,128]{1,0:T(8,128)S(1)} custom-call(f32[128,128]{1,0:T(8,128)S(1)} %convolution_subtract_fusion.8), custom_call_target="Cholesky" | custom-call | tf_op jit(solution)/shard_map/jit(cholesky)/cholesky | solution.py:25
  797.2 11.7 %while.9 = (s32[]{:T(128)}, f32[512,512]{1,0:T(8,128)}, s32[4,2]{0,1:T(2,128)S(1)}, f32[4,128,128]{2,1,0:T(8,128)S(1)}, s32[]{:T(128)}) while((s32[]{:T(128)}, f32[512,512]{1,0:T(8,128)}, s32[4,2]{0,1:T(2,128)S(1)}, f32[4,128,128]{2,1,0:T(8,128)S(1)}, s32[]{:T(128)}) %tuple.94), condition=%wide.while_cond.4.clone, body=%wide.while_body.4.clone.sunk | while | flops 2 | bytes 131181 | solution.py:15
  809.0 39.3 %custom-call.34 = f32[4,128,128]{1,2,0:T(8,128)S(1)} custom-call(f32[4,128,128]{2,1,0:T(8,128)S(1)} %get-tuple-element.70), custom_call_target="InvertDiagBlocksLowerTriangular" | custom-call | tf_op jit(solution)/shard_map/jit(_solve_triangular)/triangular_solve | solution.py:15
  861.0 64.4 %all-reduce.16.cloned.1.call-done = f32[2,512,512]{1,2,0:T(8,128)} async-done(((f32[2,512,512]{1,2,0:T(8,128)}), f32[2,512,512]{1,2,0:T(8,128)}) %all-reduce.16.cloned.1.call-update) | async-done | bytes 2097168 | tf_op jit(solution)/shard_map/psum | solution.py:9
  931.2 103.5 %all-reduce.18.cloned.1.call-done = (f32[2,1,512,512]{2,3,0,1:T(8,128)}, f32[2,1,512,512]{2,3,0,1:T(8,128)}) async-done(((f32[2,1,512,512]{2,3,0,1:T(8,128)}, f32[2,1,512,512]{2,3,0,1:T(8,128)}), (f32[2,1,512,512]{2,3,0,1:T(8,128)}, f32[2,1,512,512]{2,3,0,1:T(8,128)})) %all-reduce.18.cloned.1.call-update) | async-done | bytes 4194320 | tf_op jit(solution)/shard_map/psum | solution.py:9
  1047.9 18.0 %fusion.7 = f32[2,512,4,512]{1,3,2,0:T(8,128)S(1)} fusion(f32[2,512,4,512]{1,3,2,0:T(8,128)} %get-tuple-element.93, f32[4,512,512]{2,1,0:T(8,128)S(1)} %bitcast_select_fusion, f32[2,512,512]{1,2,0:T(8,128)S(1)} %copy-done.2, pred[2]{0:T(512)(128)(4,1)S(1)} %get-tuple-element.132), kind=kOutput, calls=%fused_computation.17 | convolution fusion | flops 12887523328 | bytes 23068674 | tf_op jit(solution)/shard_map/aur,bvr->aubv/dot_general | solution.py:44
  1072.5 20.5 %copy.88 = f32[2,1,512,4,1,512]{5,4,3,2,1,0:T(1,128)} copy(f32[2,1,512,4,1,512]{2,5,3,0,4,1:T(8,128)} %fusion.2) | data formatting | bytes 16777216 | tf_op jit(solution)/shard_map/scatter | solution.py:59
  (151 shorter events, 156.2 us)
Async XLA Ops:
  43.4 100.0 %all-to-all-start = ((f32[2,64,4,8,512]{4,2,1,0,3:T(4,128)}), f32[2,64,4,8,512]{4,2,1,0,3:T(4,128)}, u32[]{:S(2)}, u32[]{:S(2)}) async-start(f32[2,64,4,8,512]{4,2,1,0,3:T(4,128)} %copy.63), calls=%async_computation | async-start | bytes 16777216 | tf_op jit(solution)/shard_map/all_to_all | solution.py:76
  49.6 191.6 %all-reduce.10.cloned.1.call-start = ((), (), s32[]{:S(2)}) async-start(), calls=%async_computation.1 | async-start | bytes 2097152 | tf_op jit(solution)/shard_map/psum | solution.py:9
  149.2 3.4 copy-start
  154.1 309.3 %all-reduce.12.cloned.1.call-start = ((), (), s32[]{:S(2)}) async-start(), calls=%async_computation.2 | async-start | bytes 4194304 | tf_op jit(solution)/shard_map/psum | solution.py:9
  241.2 2.6 copy-start.3
  245.3 1.0 copy-start.8
  398.9 173.9 %all-reduce.20.cloned.1.call-start = ((), (), s32[]{:S(2)}) async-start(), calls=%async_computation.6 | async-start | bytes 8388608 | tf_op jit(solution)/shard_map/psum | solution.py:9
  467.8 235.0 %all-reduce.14.cloned.1.call-start = ((), (), s32[]{:S(2)}) async-start(), calls=%async_computation.3 | async-start | bytes 2097152 | tf_op jit(solution)/shard_map/psum | solution.py:9
  467.9 10.2 copy-start.5
  582.7 3.2 copy-start.1
  616.4 309.0 %all-reduce.16.cloned.1.call-start = ((), (), s32[]{:S(2)}) async-start(), calls=%async_computation.4 | async-start | bytes 4194304 | tf_op jit(solution)/shard_map/psum | solution.py:9
  702.8 2.6 copy-start.4
  706.8 1.0 copy-start.7
  860.9 173.8 %all-reduce.18.cloned.1.call-start = ((), (), s32[]{:S(2)}) async-start(), calls=%async_computation.5 | async-start | bytes 8388608 | tf_op jit(solution)/shard_map/psum | solution.py:9
  929.6 1.2 copy-start.6
  1044.7 3.2 copy-start.2
Sparse Core Ops, SparseCore 0:
  154.2 86.9 all-reduce.9
  399.0 64.3 all-reduce.11
  467.9 104.8 all-reduce.19
  616.5 86.1 all-reduce.13
  861.0 64.2 all-reduce.15
  929.8 104.8 all-reduce.17
where the time goes:
time: 1110 us; the launch traced here: 1100 us
  waiting for transfers between devices  583 us (53%)
  other arithmetic  280 us (25%)
  local copies, waits for them, and re-layouts  149 us (13%)
  matrix products  62.2 us (6%)
  between operations  19.6 us (2%)
    psum x6, waiting for transfers between devices, spread(): return lax.psum(block, axis)  489 us
    another operation x29, other arithmetic, factor(): factor_tile = jnp.linalg.cholesky(diag_tile)  158 us
    all_to_all x1, waiting for transfers between devices, shards(): lax.all_to_all(shaped, 'col', split_axis=3, concat_axis=1, tiled=True)  93.7 us
    another operation x5, other arithmetic, solve_rows(): jax.scipy.linalg.solve_triangular(factor_tile, stacked.T, lower=True)  82.2 us
    dot_general x2, matrix products, update(): jnp.einsum('aur,bvr->aubv', left_part, right_part, precision=lax.Precisio...  36 us
    reshape x1, local copies, waits for them, and re-layouts, shards(): kernel_rows.reshape(row_tiles, sub_rows, col_tiles, grid_cols, tile_size)  23.6 us
    unnamed x21, local copies, waits for them, and re-layouts  23.4 us
    another operation x27, local copies, waits for them, and re-layouts, solve_rows(): jax.scipy.linalg.solve_triangular(factor_tile, stacked.T, lower=True)  23.3 us
  transfers between devices with their start and end apart: 7, of which 7 were waited for; matrix products, arithmetic and copies ran while one was open for 2% of the time, Pallas kernels for 0%

commit v1 on v0

--- a/solution.py
+++ b/solution.py
@@ -6,7 +6,7 @@
 
 def spread(block, axis, owner):
     block = jnp.where(lax.axis_index(axis) == owner, block, jnp.zeros_like(block))
-    return lax.psum(block, axis)
+    return jnp.sum(lax.all_gather(block, axis), axis=0)
 
 
 def solve_rows(factor_tile, column):

time: 1110 us -> 1820 us (1.64)
  waiting for transfers between devices: 583 us -> 1230 us
  other arithmetic: 280 us -> 362 us
  local copies, waits for them, and re-layouts: 149 us -> 106 us
  matrix products: 62.2 us -> 88 us
    all_gather x0 -> x8, waiting for transfers between devices: none -> 1140 us  [spread(): return jnp.sum(lax.all_gather(block, axis), axis=0)]
    psum x6 -> x0, waiting for transfers between devices: 489 us -> none  [spread(): return lax.psum(block, axis)]
    reduce_sum x0 -> x8, other arithmetic: none -> 89.3 us  [spread(): return jnp.sum(lax.all_gather(block, axis), axis=0)]
    dot_general x2, matrix products: 36 us -> 61.8 us  [update(): jnp.einsum('aur,bvr->aubv', left_part, right_part, precision=lax.Precisio...]
  transfers between devices with their start and end apart: 7 -> 9, of which waited for: 7 -> 9; matrix products, arithmetic and copies ran while one was open for 2% -> 3% of each run, Pallas kernels for 0% -> 0%
where the time goes in v1:
time: 1820 us; the launch traced here: 1810 us
  waiting for transfers between devices  1230 us (68%)
  other arithmetic  362 us (20%)
  local copies, waits for them, and re-layouts  106 us (6%)
  matrix products  88 us (5%)
  between operations  19.7 us (1%)
    all_gather x8, waiting for transfers between devices, spread(): return jnp.sum(lax.all_gather(block, axis), axis=0)  1140 us
    another operation x29, other arithmetic, factor(): factor_tile = jnp.linalg.cholesky(diag_tile)  159 us
    all_to_all x1, waiting for transfers between devices, shards(): lax.all_to_all(shaped, 'col', split_axis=3, concat_axis=1, tiled=True)  93.7 us
    reduce_sum x8, other arithmetic, spread(): return jnp.sum(lax.all_gather(block, axis), axis=0)  89.3 us
    another operation x5, other arithmetic, solve_rows(): jax.scipy.linalg.solve_triangular(factor_tile, stacked.T, lower=True)  81.8 us
    dot_general x2, matrix products, update(): jnp.einsum('aur,bvr->aubv', left_part, right_part, precision=lax.Precisio...  61.8 us
  transfers between devices with their start and end apart: 9, of which 9 were waited for; matrix products, arithmetic and copies ran while one was open for 3% of the time, Pallas kernels for 0%

profile of v1, /device:TPU:1, one launch (start us, length us, event | category | flops | bytes accessed | tf_op | source)
XLA Modules:
  0.0 1814.3 jit_solution(13033943822335481092)
XLA Ops:
  6.5 9.9 copy.56
  31.1 93.7 %all-to-all-done = f32[2,64,4,8,512]{4,1,2,0,3:T(8,128)} async-done(((f32[2,64,4,8,512]{4,1,2,0,3:T(8,128)}), f32[2,64,4,8,512]{4,1,2,0,3:T(8,128)}, u32[]{:S(2)}, u32[]{:S(2)}) %all-to-all-start) | async-done | bytes 8388640 | tf_op jit(solution)/shard_map/all_to_all | solution.py:76
  138.9 107.1 %all-gather.19.cloned.1.call-done = f32[16,512,1,512]{3,1,2,0:T(8,128)} async-done(((f32[1,512,1,512]{3,1,2,0:T(8,128)}), f32[16,512,1,512]{3,1,2,0:T(8,128)}) %all-gather.19.cloned.1.call-update) | async-done | bytes 16777232 | tf_op jit(solution)/shard_map/all_gather | solution.py:9
  257.7 11.7 cholesky.286
  269.4 9.8 custom-call.27
  281.9 12.1 cholesky.305
  294.0 9.8 custom-call.28
  305.4 11.7 cholesky.326
  329.1 11.9 cholesky.343
  346.6 11.7 while.8
  358.3 39.3 %custom-call.30 = f32[4,128,128]{1,2,0:T(8,128)S(1)} custom-call(f32[4,128,128]{2,1,0:T(8,128)S(1)} %get-tuple-element.69), custom_call_target="InvertDiagBlocksLowerTriangular" | custom-call | tf_op jit(solution)/shard_map/jit(_solve_triangular)/triangular_solve | solution.py:15
  407.5 85.1 %all-gather.15.cloned.1.call-done = f32[8,2,512,512]{3,2,1,0:T(8,128)} async-done(((f32[1,2,512,512]{3,2,1,0:T(8,128)}), f32[8,2,512,512]{3,2,1,0:T(8,128)}) %all-gather.15.cloned.1.call-update) | async-done | bytes 16777232 | tf_op jit(solution)/shard_map/all_gather | solution.py:9
  516.5 193.0 %all-gather.21.cloned.1.call-done = f32[32,512,512]{2,1,0:T(8,128)} async-done(((f32[2,512,512]{2,1,0:T(8,128)}), f32[32,512,512]{2,1,0:T(8,128)}) %all-gather.21.cloned.1.call-update) | async-done | bytes 33554448 | tf_op jit(solution)/shard_map/all_gather | solution.py:9
  709.5 14.6 reduce_sum.78
  724.1 184.1 %all-gather.23.cloned.1.call-done = f32[32,512,512]{2,1,0:T(8,128)} async-done(((f32[2,512,512]{2,1,0:T(8,128)}), f32[32,512,512]{2,1,0:T(8,128)}) %all-gather.23.cloned.1.call-update) | async-done | bytes 33554448 | tf_op jit(solution)/shard_map/all_gather | solution.py:9
  908.2 14.1 reduce_sum.79
  928.1 29.1 %fusion.7 = f32[2,512,4,512]{3,1,2,0:T(8,128)} fusion(f32[2,512,4,512]{3,1,2,0:T(8,128)S(1)} %bitcast.167, f32[4,512,512]{2,1,0:T(8,128)S(1)} %bitcast_select_fusion.1, f32[2,512,512,1]{1,0,2,3:T(2,128)S(1)} %copy-done.2), kind=kOutput, calls=%fused_computation.17 | convolution fusion | flops 12886999040 | bytes 23068672 | tf_op jit(solution)/shard_map/aur,bvr->aubv/dot_general | solution.py:44
  971.9 106.0 %all-gather.25.cloned.1.call-done = f32[16,512,1,512]{3,1,2,0:T(8,128)} async-done(((f32[1,512,1,512]{3,1,2,0:T(8,128)}), f32[16,512,1,512]{3,1,2,0:T(8,128)}) %all-gather.25.cloned.1.call-update) | async-done | bytes 16777232 | tf_op jit(solution)/shard_map/all_gather | solution.py:9
  1089.6 11.7 cholesky.358
  1101.4 9.8 custom-call.31
  1113.8 12.1 cholesky.377
  1138.6 11.7 cholesky.398
  1162.3 11.9 cholesky.415
  1179.1 11.7 while.9
  1190.8 39.3 %custom-call.34 = f32[4,128,128]{1,2,0:T(8,128)S(1)} custom-call(f32[4,128,128]{2,1,0:T(8,128)S(1)} %get-tuple-element.70), custom_call_target="InvertDiagBlocksLowerTriangular" | custom-call | tf_op jit(solution)/shard_map/jit(_solve_triangular)/triangular_solve | solution.py:15
  1240.0 85.1 %all-gather.17.cloned.1.call-done = f32[8,2,512,512]{3,2,1,0:T(8,128)} async-done(((f32[1,2,512,512]{3,2,1,0:T(8,128)}), f32[8,2,512,512]{3,2,1,0:T(8,128)}) %all-gather.17.cloned.1.call-update) | async-done | bytes 16777232 | tf_op jit(solution)/shard_map/all_gather | solution.py:9
  1348.9 193.1 %all-gather.27.cloned.1.call-done = f32[32,512,512]{2,1,0:T(8,128)} async-done(((f32[2,512,512]{2,1,0:T(8,128)}), f32[32,512,512]{2,1,0:T(8,128)}) %all-gather.27.cloned.1.call-update) | async-done | bytes 33554448 | tf_op jit(solution)/shard_map/all_gather | solution.py:9
  1542.0 14.5 reduce_sum.83
  1556.5 184.3 %all-gather.29.cloned.1.call-done = f32[32,512,512]{2,1,0:T(8,128)} async-done(((f32[2,512,512]{2,1,0:T(8,128)}), f32[32,512,512]{2,1,0:T(8,128)}) %all-gather.29.cloned.1.call-update) | async-done | bytes 33554448 | tf_op jit(solution)/shard_map/all_gather | solution.py:9
  1740.9 14.1 reduce_sum.84
  1759.2 32.7 %fusion.10 = f32[2,512,4,512]{3,1,2,0:T(8,128)S(1)} fusion(f32[2,512,4,512]{3,1,2,0:T(8,128)} %get-tuple-element.89, f32[4,512,512]{2,1,0:T(8,128)S(1)} %bitcast_select_fusion, f32[2,512,512,1]{1,0,2,3:T(2,128)S(1)} %copy-done.1), kind=kOutput, calls=%fused_computation.18 | convolution fusion | flops 12886999040 | bytes 23068672 | tf_op jit(solution)/shard_map/aur,bvr->aubv/dot_general | solution.py:44
  1794.3 12.7 copy.44
  (161 shorter events, 218.4 us)
Async XLA Ops:
  24.7 100.1 %all-to-all-start = ((f32[2,64,4,8,512]{4,1,2,0,3:T(8,128)}), f32[2,64,4,8,512]{4,1,2,0,3:T(8,128)}, u32[]{:S(2)}, u32[]{:S(2)}) async-start(f32[2,64,4,8,512]{4,1,2,0,3:T(8,128)} %copy.25), calls=%async_computation | async-start | bytes 16777216 | tf_op jit(solution)/shard_map/all_to_all | solution.py:76
  31.1 214.9 %all-gather.19.cloned.1.call-start = ((), (), s32[]{:S(2)}) async-start(), calls=%async_computation.3 | async-start | bytes 17825792 | tf_op jit(solution)/shard_map/all_gather | solution.py:9
  129.3 3.4 copy-start
  133.8 358.8 %all-gather.15.cloned.1.call-start = ((), (), s32[]{:S(2)}) async-start(), calls=%async_computation.1 | async-start | bytes 18874368 | tf_op jit(solution)/shard_map/all_gather | solution.py:9
  256.7 1.0 copy-start.6
  407.4 302.1 %all-gather.21.cloned.1.call-start = ((), (), s32[]{:S(2)}) async-start(), calls=%async_computation.4 | async-start | bytes 35651584 | tf_op jit(solution)/shard_map/all_gather | solution.py:9
  512.2 396.0 %all-gather.23.cloned.1.call-start = ((), (), s32[]{:S(2)}) async-start(), calls=%async_computation.5 | async-start | bytes 35651584 | tf_op jit(solution)/shard_map/all_gather | solution.py:9
  516.4 561.4 %all-gather.25.cloned.1.call-start = ((), (), s32[]{:S(2)}) async-start(), calls=%async_computation.6 | async-start | bytes 17825792 | tf_op jit(solution)/shard_map/all_gather | solution.py:9
  922.3 3.5 slice-start
  925.1 2.3 slice-start.1
  925.1 2.9 copy-start.2
  928.1 29.1 %copy-start.3 = (f32[512,512]{1,0:T(8,128)S(1)}, f32[512,512]{1,0:T(8,128)}, u32[]{:S(2)}) copy-start(f32[512,512]{1,0:T(8,128)} %get-tuple-element.92) | copy-start | bytes 3145732
  966.8 358.3 %all-gather.17.cloned.1.call-start = ((), (), s32[]{:S(2)}) async-start(), calls=%async_computation.2 | async-start | bytes 18874368 | tf_op jit(solution)/shard_map/all_gather | solution.py:9
  1088.5 1.0 copy-start.5
  1239.9 302.1 %all-gather.27.cloned.1.call-start = ((), (), s32[]{:S(2)}) async-start(), calls=%async_computation.7 | async-start | bytes 35651584 | tf_op jit(solution)/shard_map/all_gather | solution.py:9
  1344.7 396.2 %all-gather.29.cloned.1.call-start = ((), (), s32[]{:S(2)}) async-start(), calls=%async_computation.8 | async-start | bytes 35651584 | tf_op jit(solution)/shard_map/all_gather | solution.py:9
  1757.6 1.6 copy-start.1
  1759.2 32.7 %copy-start.4 = (f32[512,512]{1,0:T(8,128)S(1)}, f32[512,512]{1,0:T(8,128)}, u32[]{:S(2)}) copy-start(f32[512,512]{1,0:T(8,128)} %get-tuple-element.88) | copy-start | bytes 3145732
Sparse Core Ops, SparseCore 0:
  133.9 112.0 all-gather.18
  407.5 84.9 all-gather.14
  512.3 197.1 all-gather.20
  711.5 196.6 all-gather.22
  966.9 110.8 all-gather.24
  1240.0 84.9 all-gather.16
  1344.8 197.1 all-gather.26
  1544.1 196.6 all-gather.28
